TPU v7x, 512 devices: a whole 4x4x16 slice. The times are simulated.
512 devices in a mesh: fsdp: 32 (over x, z_hi, core), ctx: 16 (over y, z_lo).
Axes of the slice: x: 4, y: 4, z: 16 (z_hi: 4, z_lo: 4; z = z_hi * 4 + z_lo), core: 2. Of those that a mesh axis runs over, the one named last changes fastest.
Arguments:
- features: bfloat16 [3, 16384, 8192], P(None, 'ctx', 'fsdp'), may hold values from -6 to 6
- short_taps: float32 [3, 3, 8192], P(None, None, 'fsdp'), may hold values from -3.5 to 3.5
- decay_rates: float32 [512, 16], P('fsdp'), may hold values from 1.5258789e-05 to 0.1
- mode_gains: float32 [512, 16], P('fsdp'), may hold values from -2.5 to 2.5
- cotangent: bfloat16 [16384, 8192], P('ctx', 'fsdp'), may hold values from -6 to 6
Outputs:
- mixer_output: bfloat16 [16384, 8192], P('ctx', 'fsdp')
- feature_grads: bfloat16 [3, 16384, 8192], P(None, 'ctx', 'fsdp')
- gain_grads: float32 [512, 16], P('fsdp')
- rate_grads: float32 [512, 16], P('fsdp')
All inputs are finite; a program needn't handle non-finite values.
Results may differ from a plain program's by a relative error of at most 0.0048.
Values may be sent and summed in bfloat16 or wider, within the bound.
A program may use at most 64 MiB of HBM per device.

v0:
```python
import jax
import jax.numpy as jnp
from jax import lax
from jax.sharding import PartitionSpec as P

precise = lax.Precision.HIGHEST
threepass = lax.Precision.HIGH


def passed_along(value, axis, steps):
    count = lax.axis_size(axis)
    leading, last = (max(0, -steps), min(count, count - steps))
    return lax.ppermute(value, axis, [(source, source + steps) for source in range(leading, last)])


def diagonal_sums(gram_acc):
    group_count, block_len, width_same = gram_acc.shape
    flipped = jnp.flip(gram_acc, axis=2)
    padded = jnp.concatenate([flipped, jnp.zeros_like(flipped)], axis=2)
    flattened = padded.reshape(group_count, 2 * block_len * block_len)[
        :, : block_len * (2 * block_len - 1)
    ]
    sheared = flattened.reshape(group_count, block_len, 2 * block_len - 1)
    return jnp.sum(sheared, axis=1)[:, block_len - 1 :]


def short_conv(taps_table, row_data, tokens, rim_rows, forward):
    summed = jnp.zeros((3, tokens, row_data.shape[2]), jnp.float32)
    for offset in range(taps_table.shape[1]):
        start_row = rim_rows - offset if forward else offset
        summed = (
            summed + taps_table[:, offset, None, :] * row_data[:, start_row : start_row + tokens, :]
        )
    return summed


def per_device(features, short_taps, decay_rates, mode_gains, cotangent):
    tokens = features.shape[1]
    channels = features.shape[2]
    group_count = decay_rates.shape[0]
    order_count = decay_rates.shape[1]
    members = channels // group_count
    rim_rows = short_taps.shape[1] - 1
    block_len = 128
    block_count = tokens // block_len
    ctx_count = lax.axis_size("ctx")
    ctx_index = lax.axis_index("ctx")
    earlier_rows = passed_along(features[:, tokens - rim_rows :, :], "ctx", 1)
    extended = jnp.concatenate([earlier_rows, features], axis=1)
    shaped = short_conv(short_taps, extended, tokens, rim_rows, True)
    query_part, key_part, value_part = (shaped[0], shaped[1], shaped[2])
    product = (key_part * value_part).astype(jnp.bfloat16)
    adjoint = cotangent * query_part
    grouped_z = product.reshape(tokens, group_count, members)
    grouped_e = adjoint.reshape(tokens, group_count, members)
    mode_coefs = mode_gains * jnp.sqrt(2.0 * decay_rates)
    rate_axis = decay_rates[:, :, None]
    positions = jnp.arange(tokens, dtype=jnp.float32)[None, None, :]
    decay_from = jnp.exp(-rate_axis * positions)
    end_tables = jnp.stack([jnp.flip(decay_from, 2), -jnp.flip(positions * decay_from, 2)])
    end_states = jnp.einsum(
        "kgns,sgm->kngm", end_tables, grouped_z.astype(jnp.float32), precision=threepass
    )
    start_state = jnp.einsum("gnt,tgm->ngm", decay_from, grouped_e, precision=precise)
    local_states = jnp.stack([end_states[0], end_states[1], start_state]).reshape(
        3, order_count, channels
    )
    lag_axis = jnp.arange(block_len, dtype=jnp.float32)[None, None, :]
    block_pow = jnp.exp(-rate_axis * lag_axis)
    block_after = block_pow * jnp.exp(-rate_axis)
    block_moments = jnp.stack([block_after, (lag_axis + 1.0) * block_after])
    coef_after = mode_coefs[:, :, None] * block_after
    block_ends = jnp.stack([jnp.flip(block_pow, 2), -jnp.flip(lag_axis * block_pow, 2)])
    coef_tail = mode_coefs[:, :, None] * jnp.flip(block_after, 2)
    block_span = jnp.exp(-decay_rates * block_len).T[:, :, None]
    lag_index = (
        jnp.arange(block_len, dtype=jnp.int32)[:, None]
        - jnp.arange(block_len, dtype=jnp.int32)[None, :]
    )
    lag_value = jnp.maximum(lag_index, 0).astype(jnp.float32)
    pair_pow = jnp.exp(-decay_rates[:, :, None, None] * lag_value[None, None])
    toeplitz = jnp.where(
        lag_index[None] >= 0, jnp.sum(mode_coefs[:, :, None, None] * pair_pow, axis=1), 0.0
    )
    z_blocks = grouped_z.reshape(block_count, block_len, group_count, members)
    e_blocks = grouped_e.reshape(block_count, block_len, group_count, members)

    def forward_block(carried_in, inputs):
        mode_state, lagged, first_acc, lag_acc, gram_acc = carried_in
        z_block, e_block = inputs
        z_wide = z_block.astype(jnp.float32)
        inside_part = jnp.einsum("gts,sgm->tgm", toeplitz, z_wide, precision=threepass)
        carried = jnp.einsum("gnt,ngm->tgm", coef_after, mode_state, precision=precise)
        moments = jnp.einsum("kgnt,tgm->kngm", block_moments, e_block, precision=precise)
        first_acc = first_acc + jnp.sum(moments[0] * mode_state, axis=2)
        lag_acc = lag_acc + jnp.sum(moments[0] * lagged - moments[1] * mode_state, axis=2)
        gram_acc = gram_acc + jnp.einsum("tgm,sgm->gts", e_block, z_wide, precision=precise)
        fresh_part = jnp.einsum("kgns,sgm->kngm", block_ends, z_wide, precision=threepass)
        new_lagged = block_span * lagged - block_len * block_span * mode_state + fresh_part[1]
        new_state = block_span * mode_state + fresh_part[0]
        return ((new_state, new_lagged, first_acc, lag_acc, gram_acc), inside_part + carried)

    zero_state = jnp.zeros((order_count, group_count, members), jnp.float32)
    zero_pairs = jnp.zeros((order_count, group_count), jnp.float32)
    zero_gram = jnp.zeros((group_count, block_len, block_len), jnp.float32)
    final_carry, inner_blocks = lax.scan(
        forward_block,
        (zero_state, zero_state, zero_pairs, zero_pairs, zero_gram),
        (z_blocks, e_blocks),
    )
    first_acc, lag_acc, gram_acc = (final_carry[2], final_carry[3], final_carry[4])
    lag_totals = diagonal_sums(gram_acc)
    first_local = first_acc.T + jnp.sum(lag_totals[:, None, :] * block_pow, axis=2)
    lag_local = lag_acc.T - jnp.sum(lag_totals[:, None, :] * lag_axis * block_pow, axis=2)
    device_after = decay_from * jnp.exp(-rate_axis)
    second_moment = jnp.einsum(
        "gnt,tgm->ngm", (positions + 1.0) * device_after, grouped_e, precision=precise
    )
    partial_rows = jnp.stack([first_local, lag_local]).reshape(-1, channels)
    partial_slot = jnp.zeros((order_count, channels), jnp.float32)
    partial_slot = partial_slot.at[: partial_rows.shape[0]].set(partial_rows)
    local_states = jnp.concatenate(
        [local_states, second_moment.reshape(1, order_count, channels), partial_slot[None]]
    )
    rate_cols = jnp.repeat(decay_rates.T, members, axis=1)
    everyone = lax.all_gather(local_states[None], "ctx", axis=0, tiled=True)
    device_ids = jnp.arange(ctx_count, dtype=jnp.int32)
    ahead_steps = (ctx_index - 1 - device_ids).astype(jnp.float32)[:, None, None]
    behind_steps = (device_ids - ctx_index - 1).astype(jnp.float32)[:, None, None]
    ahead_weight = jnp.where(
        ahead_steps >= 0, jnp.exp(-rate_cols[None] * (tokens * jnp.maximum(ahead_steps, 0.0))), 0.0
    )
    behind_weight = jnp.where(
        behind_steps >= 0,
        jnp.exp(-rate_cols[None] * (tokens * jnp.maximum(behind_steps, 0.0))),
        0.0,
    )
    prev_state = jnp.sum(ahead_weight * everyone[:, 0], axis=0)
    next_state = jnp.sum(behind_weight * everyone[:, 2], axis=0)
    all_ids = device_ids.astype(jnp.float32)
    pair_steps = (all_ids[:, None] - 1.0 - all_ids[None, :])[:, :, None, None]
    pair_weight = jnp.where(
        pair_steps >= 0,
        jnp.exp(-rate_cols[None, None] * (tokens * jnp.maximum(pair_steps, 0.0))),
        0.0,
    )
    all_prev = jnp.sum(pair_weight * everyone[None, :, 0], axis=1)
    all_lagged = jnp.sum(
        pair_weight * (everyone[None, :, 1] - tokens * pair_steps * everyone[None, :, 0]), axis=1
    )
    all_first = jnp.exp(-rate_cols)[None] * everyone[:, 2]
    cross_first = jnp.sum(all_first * all_prev, axis=0)
    cross_lag = jnp.sum(all_first * all_lagged - everyone[:, 3] * all_prev, axis=0)
    cross_first = cross_first.reshape(order_count, group_count, members).sum(axis=2).T
    cross_lag = cross_lag.reshape(order_count, group_count, members).sum(axis=2).T
    gathered_parts = everyone[:, 4, : partial_rows.shape[0]].reshape(
        ctx_count, 2, group_count, order_count
    )
    local_totals = jnp.sum(gathered_parts, axis=0)
    first_total = local_totals[0] + cross_first
    lag_total = local_totals[1] + cross_lag

    def backward_block(later_state, e_block):
        inside_part = jnp.einsum("gts,tgm->sgm", toeplitz, e_block, precision=precise)
        carried = jnp.einsum("gns,ngm->sgm", coef_tail, later_state, precision=precise)
        fresh_part = jnp.einsum("gnt,tgm->ngm", block_pow, e_block, precision=precise)
        return (block_span * later_state + fresh_part, inside_part + carried)

    top_state, grad_blocks = lax.scan(backward_block, zero_state, e_blocks, reverse=True)
    prev_grouped = prev_state.reshape(order_count, group_count, members)
    next_grouped = next_state.reshape(order_count, group_count, members)
    inner_sum = inner_blocks.reshape(tokens, group_count, members) + jnp.einsum(
        "gnt,ngm->tgm", mode_coefs[:, :, None] * device_after, prev_grouped, precision=precise
    )
    device_tail = mode_coefs[:, :, None] * jnp.flip(device_after, 2)
    product_grad = grad_blocks.reshape(tokens, group_count, members) + jnp.einsum(
        "gns,ngm->sgm", device_tail, next_grouped, precision=precise
    )
    gain_part = jnp.sqrt(2.0 * decay_rates) * first_total
    rate_part = mode_coefs * (0.5 * first_total + decay_rates * lag_total)
    inner_flat = inner_sum.reshape(tokens, channels)
    mixer_output = (query_part * inner_flat).astype(jnp.bfloat16)
    grad_flat = product_grad.reshape(tokens, channels)
    feature_adj = jnp.stack([cotangent * inner_flat, grad_flat * value_part, grad_flat * key_part])
    later_rows = passed_along(feature_adj[:, :rim_rows, :], "ctx", -1)
    appended = jnp.concatenate([feature_adj, later_rows], axis=1)
    feature_grads = short_conv(short_taps, appended, tokens, rim_rows, False).astype(jnp.bfloat16)
    filter_local = jnp.stack([gain_part, rate_part])
    entry_count = 2 * group_count * order_count * lax.axis_size("fsdp")
    summed = filter_local
    squares = lax.psum(jnp.sum(summed * summed), "fsdp")
    factor = jnp.minimum(1.0, lax.rsqrt(squares / entry_count + 1e-06))
    clipped = summed * factor
    return (mixer_output, feature_grads, clipped[0], clipped[1])


def solution(mesh):
    return jax.shard_map(
        per_device,
        mesh=mesh,
        in_specs=(
            P(None, "ctx", "fsdp"),
            P(None, None, "fsdp"),
            P("fsdp", None),
            P("fsdp", None),
            P("ctx", "fsdp"),
        ),
        out_specs=(P("ctx", "fsdp"), P(None, "ctx", "fsdp"), P("fsdp", None), P("fsdp", None)),
        check_vma=False,
    )
```

profile of v0, /device:TPU:1, one launch (start us, length us, event | category | flops | bytes accessed | tf_op | source)
XLA Modules:
  0.0 461.2 jit_solution(7824403788756353742)
XLA Ops:
  8.8 5.1 %collective-permute-start = (bf16[3,2,256]{1,2,0:T(8,128)(2,1)}, bf16[3,2,256]{1,2,0:T(8,128)(2,1)}, u32[]{:S(2)}, u32[]{:S(2)}) collective-permute-start(bf16[3,2,256]{1,2,0:T(8,128)(2,1)} %copy.110), channel_id=1, source_target_pairs={{0,1},{1,2},{2,3},{3,4},{4,5},{5,6},{6,7},{7,8},{8,9},{9,10},{10,1... | collective-permute-start | bytes 9224 | tf_op jit(solution)/shard_map/ppermute | solution.py:13
  17.4 1.9 fusion.72
  28.5 5.2 %multiply_reduce_fusion.1 = f32[16,128,128]{2,1,0:T(8,128)S(1)} fusion(f32[128,128]{1,0:T(8,128)S(1)} %maximum_convert_fusion, f32[16,16]{1,0:T(8,128)S(1)} %get-tuple-element.800, f32[16,16]{1,0:T(8,128)} %copy.115), kind=kLoop, calls=%fused_computation.65 | loop fusion | flops 12320768 | bytes 1116160 | tf_op jit(solution)/shard_map/reduce_sum | solution.py:83
  37.1 2.6 copy.109
  42.0 2.0 copy.112
  44.0 5.5 %rev.26 = f32[16,16,1024]{2,1,0:T(8,128)} reverse(f32[16,16,1024]{2,1,0:T(8,128)} %get-tuple-element.565), dimensions={2} | reverse | bytes 2097152 | tf_op jit(solution)/shard_map/jit(_flip)/rev | solution.py:60
  53.0 3.3 rev.30
  56.4 4.6 %multiply_add_fusion = f32[3,1024,256]{1,2,0:T(8,128)S(1)} fusion(bf16[3,1024,256]{1,2,0:T(8,128)(2,1)} %copy.109, bf16[3,2,256]{1,2,0:T(8,128)(2,1)} %collective-permute-done, f32[3,256]{1,0:T(4,128)} %get-tuple-element.575, f32[3,256]{1,0:T(4,128)} %get-tuple-element.576, f32[3,256]{1,0:T(4,128)} %bitcast.282), kind=kLoop, calls=%fused_computation.76 | loop fusion | flops 11010048 | bytes 4730880 | tf_op jit(solution)/shard_map/add | solution.py:32
  66.1 134.3 %while.39 = (s32[]{:T(128)}, f32[16,16,16]{0,2,1:T(8,128)}, f32[16,16,16]{0,2,1:T(8,128)}, f32[16,16]{0,1:T(8,128)}, f32[16,16]{0,1:T(8,128)}, /*index=5*/f32[16...) while((s32[]{:T(128)}, f32[16,16,16]{0,2,1:T(8,128)}, ...), condition=%wide.region_4.5_spmd.clone, body=%wide.region_1.4_spmd.clone.sunk | while | flops 101380864 | bytes 5014714 | solution.py:106
  68.9 2.9 convolution_bitcast_fusion.7
  74.7 4.5 dynamic_update_slice.17
  79.2 2.0 convolution_add_fusion.6
  84.3 2.9 convolution_bitcast_fusion.7
  91.7 4.5 dynamic_update_slice.17
  96.2 2.0 convolution_add_fusion.6
  101.3 2.9 convolution_bitcast_fusion.7
  104.2 1.8 fusion.139
  108.7 4.5 dynamic_update_slice.17
  113.2 2.0 convolution_add_fusion.6
  118.3 2.9 convolution_bitcast_fusion.7
  121.2 1.8 fusion.139
  125.8 4.5 dynamic_update_slice.17
  130.2 2.0 convolution_add_fusion.6
  135.3 2.9 convolution_bitcast_fusion.7
  138.2 1.8 fusion.139
  142.8 4.5 dynamic_update_slice.17
  147.3 2.0 convolution_add_fusion.6
  152.4 2.9 convolution_bitcast_fusion.7
  155.3 1.8 fusion.139
  159.8 4.5 dynamic_update_slice.17
  164.3 2.0 convolution_add_fusion.6
  169.4 2.9 convolution_bitcast_fusion.7
  176.9 4.5 dynamic_update_slice.17
  181.3 2.0 convolution_add_fusion.6
  186.4 2.9 convolution_bitcast_fusion.7
  189.3 1.8 fusion.139
  193.9 4.5 dynamic_update_slice.17
  198.3 2.0 convolution_add_fusion.6
  200.4 5.8 %rev.28 = f32[16,128,128]{2,1,0:T(8,128)} reverse(f32[16,128,128]{2,1,0:T(8,128)S(1)} %get-tuple-element.253), dimensions={2} | reverse | bytes 2097152 | tf_op jit(solution)/shard_map/jit(_flip)/rev | solution.py:18
  210.3 6.2 %reshape.321 = f32[16,128,255]{2,1,0:T(8,128)} reshape(f32[16,32640]{1,0:T(8,128)} %slice.145) | data formatting | bytes 4177920 | tf_op jit(solution)/shard_map/reshape | solution.py:23
  216.5 1.8 reduce_sum.145
  221.4 5.0 %fusion.63 = f32[2,16,16,16]{1,3,0,2:T(8,128)} fusion(bf16[1024,16,16,1]{0,2,3,1:T(8,128)(2,1)} %bitcast.272, f32[1,16,16,1024]{3,2,0,1:T(8,128)} %negate_bitcast_fusion, f32[1,16,16,1024]{3,2,0,1:T(8,128)} %bitcast.269), kind=kOutput, calls=%fused_computation.91 | convolution fusion | flops 50855936 | bytes 2654208 | tf_op jit(solution)/shard_map/kgns,sgm->kngm/dot_general | solution.py:61
  226.3 1.8 copy.123
  231.3 2.9 fusion.70
  238.5 48.9 %while.40 = (s32[]{:T(128)}, f32[16,16,16]{0,2,1:T(8,128)S(1)}, f32[8,128,16,16]{1,0,3,2:T(8,128)}, f32[16,16,1]{0,1,2:T(8,128)S(1)}, f32[8,128,16,16]{1,3,2,0:T...) while((s32[]{:T(128)}, f32[16,16,16]{0,2,1:T(8,128)S(1)}, ...), condition=%wide.region_10.11_spmd.clone, body=%wide.region_9.10_spmd.clone.sunk | while | flops 62996484 | bytes 2277520 | solution.py:169
  239.7 4.4 dynamic_update_slice.18
  245.8 4.4 dynamic_update_slice.18
  251.9 4.4 dynamic_update_slice.18
  258.0 4.4 dynamic_update_slice.18
  264.2 4.4 dynamic_update_slice.18
  270.3 4.4 dynamic_update_slice.18
  276.4 4.4 dynamic_update_slice.18
  282.5 4.4 dynamic_update_slice.18
  287.5 2.4 reshape.324
  289.9 30.7 %all-gather.3.cloned.1.call-done = f32[80,16,256]{2,1,0:T(8,128)} async-done(((f32[5,16,256]{2,1,0:T(8,128)}), f32[80,16,256]{2,1,0:T(8,128)}) %all-gather.3.cloned.1.call-update) | async-done | bytes 1310736 | tf_op jit(solution)/shard_map/all_gather | solution.py:126
  322.7 2.4 multiply_reduce_fusion.2
  326.8 2.4 reshape.317
  329.2 94.6 %psum.7 = f32[]{:T(128)} all-reduce(f32[]{:T(128)} %multiply_reduce_fusion.9), channel_id=1, replica_groups=mesh['fsdp'=32,'ctx'=16] {'fsdp'}, use_global_device_ids=true, to_apply=%region_20.21 | all-reduce | flops 1 | bytes 8 | tf_op jit(solution)/shard_map/psum | solution.py:191
  424.7 2.6 fusion.61
  429.0 2.6 fusion.62
  431.6 2.0 fusion.66
  438.5 8.5 %collective-permute-done.1 = f32[3,2,256]{1,2,0:T(8,128)S(1)} collective-permute-done((f32[3,2,256]{1,2,0:T(8,128)S(1)}, f32[3,2,256]{1,2,0:T(8,128)S(1)}, u32[]{:S(2)}, u32[]{:S(2)}) %collective-permute-start.1) | collective-permute-done | bytes 6176 | tf_op jit(solution)/shard_map/ppermute | solution.py:13
  448.5 3.3 fusion.54
  451.8 2.6 copy.139
  (243 shorter events, 118.0 us)
Async XLA Ops:
  7.2 17.1 %copy-start.34 = (f32[3,3,256]{2,1,0:T(4,128)S(1)}, f32[3,3,256]{2,1,0:T(4,128)}, u32[]{:S(2)}) copy-start(f32[3,3,256]{2,1,0:T(4,128)} %param.12) | copy-start | bytes 27652
  7.2 17.7 %copy-start.31 = (f32[16,16]{1,0:T(8,128)S(1)}, f32[16,16]{1,0:T(8,128)}, u32[]{:S(2)}) copy-start(f32[16,16]{1,0:T(8,128)} %param.14) | copy-start | bytes 3076
  7.2 313.4 %all-gather.3.cloned.1.call-start = ((), (), s32[]{:S(2)}) async-start(), calls=%async_computation | async-start | bytes 1392640 | tf_op jit(solution)/shard_map/all_gather | solution.py:126
  8.8 47.6 %collective-permute-start = (bf16[3,2,256]{1,2,0:T(8,128)(2,1)}, bf16[3,2,256]{1,2,0:T(8,128)(2,1)}, u32[]{:S(2)}, u32[]{:S(2)}) collective-permute-start(bf16[3,2,256]{1,2,0:T(8,128)(2,1)} %copy.110), channel_id=1, source_target_pairs={{0,1},{1,2},{2,3},{3,4},{4,5},{5,6},{6,7},{7,8},{8,9},{9,10},{10,1... | collective-permute-start | bytes 9224 | tf_op jit(solution)/shard_map/ppermute | solution.py:13
  15.9 9.7 %copy-start.18 = (f32[16,16]{0,1:T(8,128)}, f32[16,16]{0,1:T(8,128)S(1)}, u32[]{:S(2)}) copy-start(f32[16,16]{0,1:T(8,128)S(1)} %copy.113) | copy-start | bytes 3076
  24.9 0.7 copy-start.20
  28.4 6.1 %copy-start.13 = (f32[1,16,16,128]{3,2,1,0:T(8,128)S(1)}, f32[1,16,16,128]{3,2,1,0:T(8,128)}, u32[]{:S(2)}) copy-start(f32[1,16,16,128]{3,2,1,0:T(8,128)} %negate_bitcast_fusion.1) | copy-start | bytes 393220
  28.4 6.0 %copy-start.14 = (f32[16,16,128]{2,1,0:T(8,128)S(1)}, f32[16,16,128]{2,1,0:T(8,128)}, u32[]{:S(2)}) copy-start(f32[16,16,128]{2,1,0:T(8,128)} %rev.24) | copy-start | bytes 393220
  28.4 6.8 %copy-start.15 = (f32[1,16,16,128]{3,2,0,1:T(8,128)S(1)}, f32[1,16,16,128]{3,2,0,1:T(8,128)}, u32[]{:S(2)}) copy-start(f32[1,16,16,128]{3,2,0,1:T(8,128)} %get-tuple-element.558) | copy-start | bytes 393220
  28.4 6.8 %copy-start.16 = (f32[1,16,16,128]{3,2,0,1:T(8,128)S(1)}, f32[1,16,16,128]{3,2,0,1:T(8,128)}, u32[]{:S(2)}) copy-start(f32[1,16,16,128]{3,2,0,1:T(8,128)} %get-tuple-element.559) | copy-start | bytes 393220
  28.4 7.5 %copy-start.29 = (f32[3,1,256]{2,1,0:T(1,128)S(1)}, f32[3,1,256]{2,1,0:T(1,128)}, u32[]{:S(2)}) copy-start(f32[3,1,256]{2,1,0:T(1,128)} %get-tuple-element.561) | copy-start | bytes 9220
  28.4 7.5 %copy-start.30 = (f32[3,1,256]{2,1,0:T(1,128)S(1)}, f32[3,1,256]{2,1,0:T(1,128)}, u32[]{:S(2)}) copy-start(f32[3,1,256]{2,1,0:T(1,128)} %get-tuple-element.562) | copy-start | bytes 9220
  28.4 8.1 %copy-start.23 = (pred[128,128]{1,0:T(8,128)(4,1)S(1)}, pred[128,128]{1,0:T(8,128)(4,1)}, u32[]{:S(2)}) copy-start(pred[128,128]{1,0:T(8,128)(4,1)} %fusion.89) | copy-start | bytes 49156
  35.2 6.2 %copy-start.28 = (f32[3,1,256]{2,1,0:T(1,128)S(1)}, f32[3,1,256]{2,1,0:T(1,128)}, u32[]{:S(2)}) copy-start(f32[3,1,256]{2,1,0:T(1,128)} %get-tuple-element.560) | copy-start | bytes 9220
  37.1 12.4 %copy-start.27 = (f32[16,16]{0,1:T(8,128)S(1)}, f32[16,16]{0,1:T(8,128)}, u32[]{:S(2)}) copy-start(f32[16,16]{0,1:T(8,128)} %get-tuple-element.569) | copy-start | bytes 3076
  61.0 1.8 copy-start
  61.0 1.4 copy-start.10
  62.8 1.0 copy-start.8
  216.5 13.3 %copy-start.9 = (f32[1024,256]{0,1:T(8,128)S(1)}, f32[1024,256]{0,1:T(8,128)}, u32[]{:S(2)}) copy-start(f32[1024,256]{0,1:T(8,128)} %copy-done.8) | copy-start | bytes 3145732
  287.4 35.3 %copy-start.17 = (f32[16,256]{1,0:T(8,128)S(1)}, f32[16,256]{1,0:T(8,128)}, u32[]{:S(2)}) copy-start(f32[16,256]{1,0:T(8,128)} %neg.43) | copy-start | bytes 49156
  287.4 35.3 %copy-start.32 = (f32[16,16]{1,0:T(8,128)S(1)}, f32[16,16]{1,0:T(8,128)}, u32[]{:S(2)}) copy-start(f32[16,16]{1,0:T(8,128)} %get-tuple-element.573) | copy-start | bytes 3076
  287.4 35.3 %copy-start.33 = (f32[16,16]{1,0:T(8,128)S(1)}, f32[16,16]{1,0:T(8,128)}, u32[]{:S(2)}) copy-start(f32[16,16]{1,0:T(8,128)} %get-tuple-element.574) | copy-start | bytes 3076
  287.4 35.3 %copy-start.39 = (pred[16,16]{1,0:T(8,128)(4,1)S(1)}, pred[16,16]{1,0:T(8,128)(4,1)}, u32[]{:S(2)}) copy-start(pred[16,16]{1,0:T(8,128)(4,1)} %subtract_compare_fusion) | copy-start | bytes 772
  287.4 37.7 %copy-start.22 = (f32[16,256]{1,0:T(8,128)S(1)}, f32[16,256]{1,0:T(8,128)}, u32[]{:S(2)}) copy-start(f32[16,256]{1,0:T(8,128)} %exp.54) | copy-start | bytes 49156
  287.4 37.7 %copy-start.35 = (f32[16]{0:T(128)S(1)}, f32[16]{0:T(128)}, u32[]{:S(2)}) copy-start(f32[16]{0:T(128)} %get-tuple-element.577) | copy-start | bytes 196
  287.4 37.7 %copy-start.36 = (f32[16]{0:T(128)S(1)}, f32[16]{0:T(128)}, u32[]{:S(2)}) copy-start(f32[16]{0:T(128)} %get-tuple-element.578) | copy-start | bytes 196
  287.4 37.7 %copy-start.37 = (pred[16]{0:T(512)(128)(4,1)S(1)}, pred[16]{0:T(512)(128)(4,1)}, u32[]{:S(2)}) copy-start(pred[16]{0:T(512)(128)(4,1)} %get-tuple-element.579) | copy-start | bytes 52
  287.4 37.7 %copy-start.38 = (pred[16]{0:T(512)(128)(4,1)S(1)}, pred[16]{0:T(512)(128)(4,1)}, u32[]{:S(2)}) copy-start(pred[16]{0:T(512)(128)(4,1)} %get-tuple-element.580) | copy-start | bytes 52
  287.5 38.7 %copy-start.19 = (f32[16,16]{0,1:T(8,128)S(1)}, f32[16,16]{0,1:T(8,128)}, u32[]{:S(2)}) copy-start(f32[16,16]{0,1:T(8,128)} %copy-done.18) | copy-start | bytes 3076
  287.5 38.7 %copy-start.21 = (f32[16,16]{0,1:T(8,128)S(1)}, f32[16,16]{0,1:T(8,128)}, u32[]{:S(2)}) copy-start(f32[16,16]{0,1:T(8,128)} %copy-done.20) | copy-start | bytes 3076
  320.5 4.6 %copy-start.12 = (f32[80,16,256]{2,1,0:T(8,128)S(1)}, f32[80,16,256]{2,1,0:T(8,128)}, u32[]{:S(2)}) copy-start(f32[80,16,256]{2,1,0:T(8,128)} %all-gather.3.cloned.1.call-done) | copy-start | bytes 3932164
  325.4 101.9 %copy-start.1 = (f32[3,1024,256]{1,2,0:T(8,128)S(1)}, f32[3,1024,256]{1,2,0:T(8,128)}, u32[]{:S(2)}) copy-start(f32[3,1024,256]{1,2,0:T(8,128)} %copy-done) | copy-start | bytes 9437188
  429.0 4.7 %copy-start.2 = (f32[1,1024,256]{1,2,0:T(8,128)S(1)}, f32[1,1024,256]{1,2,0:T(8,128)}, u32[]{:S(2)}) copy-start(f32[1,1024,256]{1,2,0:T(8,128)} %get-tuple-element.546) | copy-start | bytes 3145732
  429.0 4.7 %copy-start.4 = (f32[1,1024,256]{1,2,0:T(8,128)S(1)}, f32[1,1024,256]{1,2,0:T(8,128)}, u32[]{:S(2)}) copy-start(f32[1,1024,256]{1,2,0:T(8,128)} %get-tuple-element.547) | copy-start | bytes 3145732
  433.7 1.0 copy-start.6
  433.7 3.8 copy-start.11
  433.7 13.3 %copy-start.3 = (f32[1,1024,256]{1,2,0:T(8,128)S(1)}, f32[1,1024,256]{1,2,0:T(8,128)}, u32[]{:S(2)}) copy-start(f32[1,1024,256]{1,2,0:T(8,128)} %get-tuple-element.546) | copy-start | bytes 3145732
  433.7 13.3 %copy-start.5 = (f32[1,1024,256]{1,2,0:T(8,128)S(1)}, f32[1,1024,256]{1,2,0:T(8,128)}, u32[]{:S(2)}) copy-start(f32[1,1024,256]{1,2,0:T(8,128)} %get-tuple-element.547) | copy-start | bytes 3145732
  434.8 12.3 %collective-permute-start.1 = (f32[3,2,256]{1,2,0:T(8,128)S(1)}, f32[3,2,256]{1,2,0:T(8,128)S(1)}, u32[]{:S(2)}, u32[]{:S(2)}) collective-permute-start(f32[3,2,256]{1,2,0:T(8,128)S(1)} %slice.149), channel_id=1, source_target_pairs={{1,0},{2,1},{3,2},{4,3},{5,4},{6,5},{7,6},{8,7},{9,8},{10,9},{11,1... | collective-permute-start | bytes 18440 | tf_op jit(solution)/shard_map/ppermute | solution.py:13
  438.5 10.0 %copy-start.7 = (f32[1,1024,256]{1,2,0:T(8,128)S(1)}, f32[1,1024,256]{1,2,0:T(8,128)}, u32[]{:S(2)}) copy-start(f32[1,1024,256]{1,2,0:T(8,128)} %copy-done.6) | copy-start | bytes 3145732
  438.5 10.0 %copy-start.24 = (f32[3,256]{1,0:T(4,128)S(1)}, f32[3,256]{1,0:T(4,128)}, u32[]{:S(2)}) copy-start(f32[3,256]{1,0:T(4,128)} %get-tuple-element.575) | copy-start | bytes 9220
  438.5 10.0 %copy-start.25 = (f32[3,256]{1,0:T(4,128)S(1)}, f32[3,256]{1,0:T(4,128)}, u32[]{:S(2)}) copy-start(f32[3,256]{1,0:T(4,128)} %get-tuple-element.576) | copy-start | bytes 9220
  438.5 10.0 %copy-start.26 = (f32[3,1,256]{2,0,1:T(4,128)S(1)}, f32[3,1,256]{2,0,1:T(4,128)}, u32[]{:S(2)}) copy-start(f32[3,1,256]{2,0,1:T(4,128)} %copy.183) | copy-start | bytes 9220
Sparse Core Ops, SparseCore 0:
  237.5 83.0 all-gather.2
where the time goes:
time: 465 us; the launch traced here: 461 us
  local copies, waits for them, and re-layouts  136 us (29%)
  matrix products  103 us (22%)
  blocking collectives  94.6 us (20%)
  other arithmetic  66.3 us (14%)
  waiting for transfers between devices  39.2 us (8%)
  between operations  15.4 us (3%)
  starting transfers between devices  6.51 us (1%)
    psum x1, blocking collectives, per_device(): squares = lax.psum(jnp.sum(summed * summed), 'fsdp')  94.6 us
    dynamic_update_slice x16, local copies, waits for them, and re-layouts, per_device(): lax.scan(forward_block, (zero_state, zero_state, zero_pairs, zero_pairs,...  71.2 us
    all_gather x1, waiting for transfers between devices, per_device(): everyone = lax.all_gather(local_states[None], 'ctx', axis=0, tiled=True)  30.7 us
    dot_general x8, matrix products, forward_block(): jnp.einsum('kgnt,tgm->kngm', block_moments, e_block, precision=precise)  23.1 us
    unnamed x96, local copies, waits for them, and re-layouts  17.8 us
    dot_general x8, matrix products, forward_block(): jnp.einsum('tgm,sgm->gts', e_block, z_wide, precision=precise)  16.3 us
    dot_general x8, matrix products, forward_block(): jnp.einsum('kgns,sgm->kngm', block_ends, z_wide, precision=threepass)  13.8 us
    reduce_sum x8, other arithmetic, forward_block(): jnp.sum(moments[0] * lagged - moments[1] * mode_state, axis=2)  13.1 us
  transfers between devices with their start and end apart: 3, of which 2 were waited for; matrix products, arithmetic and copies ran while one was open for 21% of the time, Pallas kernels for 0%

commit v1 on v0

--- a/solution.py
+++ b/solution.py
@@ -123,7 +123,9 @@
         [local_states, second_moment.reshape(1, order_count, channels), partial_slot[None]]
     )
     rate_cols = jnp.repeat(decay_rates.T, members, axis=1)
-    everyone = lax.all_gather(local_states[None], "ctx", axis=0, tiled=True)
+    everyone = jnp.concatenate(
+        lax.all_to_all(jnp.stack([local_states[None]] * lax.axis_size("ctx")), "ctx", 0, 0), axis=0
+    )
     device_ids = jnp.arange(ctx_count, dtype=jnp.int32)
     ahead_steps = (ctx_index - 1 - device_ids).astype(jnp.float32)[:, None, None]
     behind_steps = (device_ids - ctx_index - 1).astype(jnp.float32)[:, None, None]

time: 465 us -> 430 us (0.925)
  the two profiles are of different devices: /device:TPU:1 before, /device:TPU:96 now
where the time goes in v1:
time: 430 us; the launch traced here: 426 us
  local copies, waits for them, and re-layouts  138 us (32%)
  matrix products  103 us (24%)
  blocking collectives  95.5 us (22%)
  other arithmetic  65.7 us (15%)
  starting transfers between devices  13.1 us (3%)
  waiting for transfers between devices  7.89 us (2%)
    psum x1, blocking collectives, per_device(): squares = lax.psum(jnp.sum(summed * summed), 'fsdp')  95.5 us
    dynamic_update_slice x16, local copies, waits for them, and re-layouts, per_device(): lax.scan(forward_block, (zero_state, zero_state, zero_pairs, zero_pairs,...  71.3 us
    dot_general x8, matrix products, forward_block(): jnp.einsum('kgnt,tgm->kngm', block_moments, e_block, precision=precise)  23.1 us
    unnamed x94, local copies, waits for them, and re-layouts  17.8 us
    dot_general x8, matrix products, forward_block(): jnp.einsum('tgm,sgm->gts', e_block, z_wide, precision=precise)  16.3 us
    dot_general x8, matrix products, forward_block(): jnp.einsum('kgns,sgm->kngm', block_ends, z_wide, precision=threepass)  13.8 us
    reduce_sum x8, other arithmetic, forward_block(): jnp.sum(moments[0] * lagged - moments[1] * mode_state, axis=2)  13 us
    dot_general x8, matrix products, forward_block(): jnp.einsum('gts,sgm->tgm', toeplitz, z_wide, precision=threepass)  11.9 us
  transfers between devices with their start and end apart: 3, of which 1 were waited for; matrix products, arithmetic and copies ran while one was open for 23% of the time, Pallas kernels for 0%

profile of v1, /device:TPU:96, one launch (start us, length us, event | category | flops | bytes accessed | tf_op | source)
XLA Modules:
  0.0 426.0 jit_solution(16456087855170264065)
XLA Ops:
  2.2 2.1 collective-permute-start
  8.5 1.9 fusion.72
  19.7 5.3 %multiply_reduce_fusion.1 = f32[16,128,128]{2,1,0:T(8,128)S(1)} fusion(f32[128,128]{1,0:T(8,128)} %maximum_convert_fusion, f32[16,16]{1,0:T(8,128)S(1)} %get-tuple-element.828, f32[16,16]{1,0:T(8,128)} %copy.132), kind=kLoop, calls=%fused_computation.65 | loop fusion | flops 12320768 | bytes 1116160 | tf_op jit(solution)/shard_map/reduce_sum | solution.py:83
  28.6 2.6 copy.126
  33.4 2.0 copy.129
  35.5 5.5 %rev.26 = f32[16,16,1024]{2,1,0:T(8,128)} reverse(f32[16,16,1024]{2,1,0:T(8,128)} %get-tuple-element.593), dimensions={2} | reverse | bytes 2097152 | tf_op jit(solution)/shard_map/jit(_flip)/rev | solution.py:60
  44.5 3.3 rev.30
  47.8 4.7 %multiply_add_fusion = f32[3,1024,256]{1,2,0:T(8,128)S(1)} fusion(bf16[3,1024,256]{1,2,0:T(8,128)(2,1)} %copy.126, bf16[3,2,256]{1,2,0:T(8,128)(2,1)} %collective-permute-done, f32[3,256]{1,0:T(4,128)} %get-tuple-element.603, f32[3,256]{1,0:T(4,128)} %get-tuple-element.604, f32[3,256]{1,0:T(4,128)} %bitcast.278), kind=kLoop, calls=%fused_computation.76 | loop fusion | flops 11010048 | bytes 4730880 | tf_op jit(solution)/shard_map/add | solution.py:32
  57.6 134.3 %while.39 = (s32[]{:T(128)}, f32[16,16,16]{0,2,1:T(8,128)}, f32[16,16,16]{0,2,1:T(8,128)}, f32[16,16]{0,1:T(8,128)}, f32[16,16]{0,1:T(8,128)}, /*index=5*/f32[16...) while((s32[]{:T(128)}, f32[16,16,16]{0,2,1:T(8,128)}, ...), condition=%wide.region_4.5_spmd.clone, body=%wide.region_1.4_spmd.clone.sunk | while | flops 101380864 | bytes 5014714 | solution.py:106
  60.4 2.9 convolution_bitcast_fusion.7
  66.2 4.5 %dynamic_update_slice.17 = f32[8,128,16,16]{1,0,3,2:T(8,128)} dynamic-update-slice(f32[8,128,16,16]{1,0,3,2:T(8,128)} %get-tuple-element.791, f32[1,128,16,16]{1,0,3,2:T(1,128)S(1)} %bitcast.257, s32[]{:T(128)} %get-tuple-element.785, s32[]{:T(128)} %constant.108.clone.1..sunk, s32[]{:T(128)} %constant.108.clone.1..sunk, s32[]{:T(128)} %constant.108.clone.1..sunk) | dynamic-update-slice | bytes 262148 | tf_op jit(solution)/shard_map/while/body/jit(dynamic_update_index_in_dim)/dynamic_update_slice | solution.py:106
  70.7 2.0 convolution_add_fusion.6
  75.8 2.9 convolution_bitcast_fusion.7
  78.7 1.8 fusion.139
  83.2 4.5 %dynamic_update_slice.17 = f32[8,128,16,16]{1,0,3,2:T(8,128)} dynamic-update-slice(f32[8,128,16,16]{1,0,3,2:T(8,128)} %get-tuple-element.791, f32[1,128,16,16]{1,0,3,2:T(1,128)S(1)} %bitcast.257, s32[]{:T(128)} %get-tuple-element.785, s32[]{:T(128)} %constant.108.clone.1..sunk, s32[]{:T(128)} %constant.108.clone.1..sunk, s32[]{:T(128)} %constant.108.clone.1..sunk) | dynamic-update-slice | bytes 262148 | tf_op jit(solution)/shard_map/while/body/jit(dynamic_update_index_in_dim)/dynamic_update_slice | solution.py:106
  87.7 2.0 convolution_add_fusion.6
  92.8 2.9 convolution_bitcast_fusion.7
  95.7 1.8 fusion.139
  100.3 4.5 %dynamic_update_slice.17 = f32[8,128,16,16]{1,0,3,2:T(8,128)} dynamic-update-slice(f32[8,128,16,16]{1,0,3,2:T(8,128)} %get-tuple-element.791, f32[1,128,16,16]{1,0,3,2:T(1,128)S(1)} %bitcast.257, s32[]{:T(128)} %get-tuple-element.785, s32[]{:T(128)} %constant.108.clone.1..sunk, s32[]{:T(128)} %constant.108.clone.1..sunk, s32[]{:T(128)} %constant.108.clone.1..sunk) | dynamic-update-slice | bytes 262148 | tf_op jit(solution)/shard_map/while/body/jit(dynamic_update_index_in_dim)/dynamic_update_slice | solution.py:106
  104.7 2.0 convolution_add_fusion.6
  109.8 2.9 convolution_bitcast_fusion.7
  112.7 1.8 fusion.139
  117.3 4.5 %dynamic_update_slice.17 = f32[8,128,16,16]{1,0,3,2:T(8,128)} dynamic-update-slice(f32[8,128,16,16]{1,0,3,2:T(8,128)} %get-tuple-element.791, f32[1,128,16,16]{1,0,3,2:T(1,128)S(1)} %bitcast.257, s32[]{:T(128)} %get-tuple-element.785, s32[]{:T(128)} %constant.108.clone.1..sunk, s32[]{:T(128)} %constant.108.clone.1..sunk, s32[]{:T(128)} %constant.108.clone.1..sunk) | dynamic-update-slice | bytes 262148 | tf_op jit(solution)/shard_map/while/body/jit(dynamic_update_index_in_dim)/dynamic_update_slice | solution.py:106
  121.7 2.0 convolution_add_fusion.6
  126.9 2.9 convolution_bitcast_fusion.7
  129.8 1.8 fusion.139
  134.3 4.5 %dynamic_update_slice.17 = f32[8,128,16,16]{1,0,3,2:T(8,128)} dynamic-update-slice(f32[8,128,16,16]{1,0,3,2:T(8,128)} %get-tuple-element.791, f32[1,128,16,16]{1,0,3,2:T(1,128)S(1)} %bitcast.257, s32[]{:T(128)} %get-tuple-element.785, s32[]{:T(128)} %constant.108.clone.1..sunk, s32[]{:T(128)} %constant.108.clone.1..sunk, s32[]{:T(128)} %constant.108.clone.1..sunk) | dynamic-update-slice | bytes 262148 | tf_op jit(solution)/shard_map/while/body/jit(dynamic_update_index_in_dim)/dynamic_update_slice | solution.py:106
  138.8 2.0 convolution_add_fusion.6
  143.9 2.9 convolution_bitcast_fusion.7
  151.3 4.5 %dynamic_update_slice.17 = f32[8,128,16,16]{1,0,3,2:T(8,128)} dynamic-update-slice(f32[8,128,16,16]{1,0,3,2:T(8,128)} %get-tuple-element.791, f32[1,128,16,16]{1,0,3,2:T(1,128)S(1)} %bitcast.257, s32[]{:T(128)} %get-tuple-element.785, s32[]{:T(128)} %constant.108.clone.1..sunk, s32[]{:T(128)} %constant.108.clone.1..sunk, s32[]{:T(128)} %constant.108.clone.1..sunk) | dynamic-update-slice | bytes 262148 | tf_op jit(solution)/shard_map/while/body/jit(dynamic_update_index_in_dim)/dynamic_update_slice | solution.py:106
  155.8 2.0 convolution_add_fusion.6
  160.9 2.9 convolution_bitcast_fusion.7
  168.4 4.5 %dynamic_update_slice.17 = f32[8,128,16,16]{1,0,3,2:T(8,128)} dynamic-update-slice(f32[8,128,16,16]{1,0,3,2:T(8,128)} %get-tuple-element.791, f32[1,128,16,16]{1,0,3,2:T(1,128)S(1)} %bitcast.257, s32[]{:T(128)} %get-tuple-element.785, s32[]{:T(128)} %constant.108.clone.1..sunk, s32[]{:T(128)} %constant.108.clone.1..sunk, s32[]{:T(128)} %constant.108.clone.1..sunk) | dynamic-update-slice | bytes 262148 | tf_op jit(solution)/shard_map/while/body/jit(dynamic_update_index_in_dim)/dynamic_update_slice | solution.py:106
  172.8 2.0 convolution_add_fusion.6
  177.9 2.9 convolution_bitcast_fusion.7
  185.4 4.5 %dynamic_update_slice.17 = f32[8,128,16,16]{1,0,3,2:T(8,128)} dynamic-update-slice(f32[8,128,16,16]{1,0,3,2:T(8,128)} %get-tuple-element.791, f32[1,128,16,16]{1,0,3,2:T(1,128)S(1)} %bitcast.257, s32[]{:T(128)} %get-tuple-element.785, s32[]{:T(128)} %constant.108.clone.1..sunk, s32[]{:T(128)} %constant.108.clone.1..sunk, s32[]{:T(128)} %constant.108.clone.1..sunk) | dynamic-update-slice | bytes 262148 | tf_op jit(solution)/shard_map/while/body/jit(dynamic_update_index_in_dim)/dynamic_update_slice | solution.py:106
  189.9 2.0 convolution_add_fusion.6
  191.9 5.8 %rev.28 = f32[16,128,128]{2,1,0:T(8,128)} reverse(f32[16,128,128]{2,1,0:T(8,128)S(1)} %get-tuple-element.253), dimensions={2} | reverse | bytes 2097152 | tf_op jit(solution)/shard_map/jit(_flip)/rev | solution.py:18
  201.9 6.2 %reshape.326 = f32[16,128,255]{2,1,0:T(8,128)} reshape(f32[16,32640]{1,0:T(8,128)} %slice.145) | data formatting | bytes 4177920 | tf_op jit(solution)/shard_map/reshape | solution.py:23
  208.1 1.8 reduce_sum.145
  212.9 5.0 %fusion.63 = f32[2,16,16,16]{1,3,0,2:T(8,128)} fusion(bf16[1024,16,16,1]{0,2,3,1:T(8,128)(2,1)} %bitcast.271, f32[1,16,16,1024]{3,2,0,1:T(8,128)} %negate_bitcast_fusion, f32[1,16,16,1024]{3,2,0,1:T(8,128)} %bitcast.268), kind=kOutput, calls=%fused_computation.92 | convolution fusion | flops 50855936 | bytes 2654208 | tf_op jit(solution)/shard_map/kgns,sgm->kngm/dot_general | solution.py:61
  217.9 1.8 copy.140
  222.9 2.9 fusion.70
  229.5 8.5 %all-to-all-start = ((f32[16,1,5,16,256]{4,3,2,1,0:T(8,128)}), f32[16,1,5,16,256]{4,3,2,1,0:T(8,128)}, u32[]{:S(2)}, u32[]{:S(2)}) async-start(f32[16,1,5,16,256]{4,3,2,1,0:T(8,128)} %stack.71), calls=%async_computation | async-start | bytes 2621440 | tf_op jit(solution)/shard_map/all_to_all | solution.py:127
  239.2 48.9 %while.40 = (s32[]{:T(128)}, f32[16,16,16]{0,2,1:T(8,128)S(1)}, f32[8,128,16,16]{1,0,3,2:T(8,128)}, f32[16,16,1]{0,1,2:T(8,128)S(1)}, f32[8,128,16,16]{1,3,2,0:T...) while((s32[]{:T(128)}, f32[16,16,16]{0,2,1:T(8,128)S(1)}, ...), condition=%wide.region_10.11_spmd.clone, body=%wide.region_9.10_spmd.clone.sunk | while | flops 62996484 | bytes 2277520 | solution.py:171
  240.4 4.4 %dynamic_update_slice.18 = f32[8,128,16,16]{1,0,3,2:T(8,128)} dynamic-update-slice(f32[8,128,16,16]{1,0,3,2:T(8,128)} %get-tuple-element.834, f32[1,128,16,16]{1,0,3,2:T(1,128)S(1)} %bitcast.258, s32[]{:T(128)S(6)} %sub.210, s32[]{:T(128)} %constant.108.clone.1..sunk.1, s32[]{:T(128)} %constant.108.clone.1..sunk.1, s32[]{:T(128)} %constant.108.clone.1..sunk.1) | dynamic-update-slice | bytes 262148 | tf_op jit(solution)/shard_map/while/body/jit(dynamic_update_index_in_dim)/dynamic_update_slice | solution.py:106
  246.5 4.4 %dynamic_update_slice.18 = f32[8,128,16,16]{1,0,3,2:T(8,128)} dynamic-update-slice(f32[8,128,16,16]{1,0,3,2:T(8,128)} %get-tuple-element.834, f32[1,128,16,16]{1,0,3,2:T(1,128)S(1)} %bitcast.258, s32[]{:T(128)S(6)} %sub.210, s32[]{:T(128)} %constant.108.clone.1..sunk.1, s32[]{:T(128)} %constant.108.clone.1..sunk.1, s32[]{:T(128)} %constant.108.clone.1..sunk.1) | dynamic-update-slice | bytes 262148 | tf_op jit(solution)/shard_map/while/body/jit(dynamic_update_index_in_dim)/dynamic_update_slice | solution.py:106
  252.7 4.4 %dynamic_update_slice.18 = f32[8,128,16,16]{1,0,3,2:T(8,128)} dynamic-update-slice(f32[8,128,16,16]{1,0,3,2:T(8,128)} %get-tuple-element.834, f32[1,128,16,16]{1,0,3,2:T(1,128)S(1)} %bitcast.258, s32[]{:T(128)S(6)} %sub.210, s32[]{:T(128)} %constant.108.clone.1..sunk.1, s32[]{:T(128)} %constant.108.clone.1..sunk.1, s32[]{:T(128)} %constant.108.clone.1..sunk.1) | dynamic-update-slice | bytes 262148 | tf_op jit(solution)/shard_map/while/body/jit(dynamic_update_index_in_dim)/dynamic_update_slice | solution.py:106
  258.8 4.4 %dynamic_update_slice.18 = f32[8,128,16,16]{1,0,3,2:T(8,128)} dynamic-update-slice(f32[8,128,16,16]{1,0,3,2:T(8,128)} %get-tuple-element.834, f32[1,128,16,16]{1,0,3,2:T(1,128)S(1)} %bitcast.258, s32[]{:T(128)S(6)} %sub.210, s32[]{:T(128)} %constant.108.clone.1..sunk.1, s32[]{:T(128)} %constant.108.clone.1..sunk.1, s32[]{:T(128)} %constant.108.clone.1..sunk.1) | dynamic-update-slice | bytes 262148 | tf_op jit(solution)/shard_map/while/body/jit(dynamic_update_index_in_dim)/dynamic_update_slice | solution.py:106
  264.9 4.4 %dynamic_update_slice.18 = f32[8,128,16,16]{1,0,3,2:T(8,128)} dynamic-update-slice(f32[8,128,16,16]{1,0,3,2:T(8,128)} %get-tuple-element.834, f32[1,128,16,16]{1,0,3,2:T(1,128)S(1)} %bitcast.258, s32[]{:T(128)S(6)} %sub.210, s32[]{:T(128)} %constant.108.clone.1..sunk.1, s32[]{:T(128)} %constant.108.clone.1..sunk.1, s32[]{:T(128)} %constant.108.clone.1..sunk.1) | dynamic-update-slice | bytes 262148 | tf_op jit(solution)/shard_map/while/body/jit(dynamic_update_index_in_dim)/dynamic_update_slice | solution.py:106
  271.0 4.4 %dynamic_update_slice.18 = f32[8,128,16,16]{1,0,3,2:T(8,128)} dynamic-update-slice(f32[8,128,16,16]{1,0,3,2:T(8,128)} %get-tuple-element.834, f32[1,128,16,16]{1,0,3,2:T(1,128)S(1)} %bitcast.258, s32[]{:T(128)S(6)} %sub.210, s32[]{:T(128)} %constant.108.clone.1..sunk.1, s32[]{:T(128)} %constant.108.clone.1..sunk.1, s32[]{:T(128)} %constant.108.clone.1..sunk.1) | dynamic-update-slice | bytes 262148 | tf_op jit(solution)/shard_map/while/body/jit(dynamic_update_index_in_dim)/dynamic_update_slice | solution.py:106
  277.1 4.4 %dynamic_update_slice.18 = f32[8,128,16,16]{1,0,3,2:T(8,128)} dynamic-update-slice(f32[8,128,16,16]{1,0,3,2:T(8,128)} %get-tuple-element.834, f32[1,128,16,16]{1,0,3,2:T(1,128)S(1)} %bitcast.258, s32[]{:T(128)S(6)} %sub.210, s32[]{:T(128)} %constant.108.clone.1..sunk.1, s32[]{:T(128)} %constant.108.clone.1..sunk.1, s32[]{:T(128)} %constant.108.clone.1..sunk.1) | dynamic-update-slice | bytes 262148 | tf_op jit(solution)/shard_map/while/body/jit(dynamic_update_index_in_dim)/dynamic_update_slice | solution.py:106
  283.2 4.4 %dynamic_update_slice.18 = f32[8,128,16,16]{1,0,3,2:T(8,128)} dynamic-update-slice(f32[8,128,16,16]{1,0,3,2:T(8,128)} %get-tuple-element.834, f32[1,128,16,16]{1,0,3,2:T(1,128)S(1)} %bitcast.258, s32[]{:T(128)S(6)} %sub.210, s32[]{:T(128)} %constant.108.clone.1..sunk.1, s32[]{:T(128)} %constant.108.clone.1..sunk.1, s32[]{:T(128)} %constant.108.clone.1..sunk.1) | dynamic-update-slice | bytes 262148 | tf_op jit(solution)/shard_map/while/body/jit(dynamic_update_index_in_dim)/dynamic_update_slice | solution.py:106
  288.1 2.4 reshape.330
  292.1 2.2 multiply_reduce_fusion.2
  296.1 2.4 reshape.322
  298.4 95.5 %psum.7 = f32[]{:T(128)} all-reduce(f32[]{:T(128)} %multiply_reduce_fusion.9), channel_id=1, replica_groups=mesh['fsdp'=32,'ctx'=16] {'fsdp'}, use_global_device_ids=true, to_apply=%region_20.21 | all-reduce | flops 1 | bytes 8 | tf_op jit(solution)/shard_map/psum | solution.py:193
  394.8 2.6 fusion.61
  399.2 2.6 fusion.62
  401.9 2.0 fusion.66
  405.7 2.4 collective-permute-start.1
  410.5 7.9 %collective-permute-done.1 = f32[3,2,256]{1,2,0:T(8,128)} collective-permute-done((f32[3,2,256]{1,2,0:T(8,128)}, f32[3,2,256]{1,2,0:T(8,128)}, u32[]{:S(2)}, u32[]{:S(2)}) %collective-permute-start.1) | collective-permute-done | bytes 6176 | tf_op jit(solution)/shard_map/ppermute | solution.py:13
  420.1 3.3 fusion.54
  423.4 2.6 copy.154
  (242 shorter events, 120.1 us)
Async XLA Ops:
  0.6 14.8 %copy-start.33 = (f32[3,3,256]{2,1,0:T(4,128)S(1)}, f32[3,3,256]{2,1,0:T(4,128)}, u32[]{:S(2)}) copy-start(f32[3,3,256]{2,1,0:T(4,128)} %param.12) | copy-start | bytes 27652
  0.6 15.4 %copy-start.30 = (f32[16,16]{1,0:T(8,128)S(1)}, f32[16,16]{1,0:T(8,128)}, u32[]{:S(2)}) copy-start(f32[16,16]{1,0:T(8,128)} %param.14) | copy-start | bytes 3076
  2.2 45.6 %collective-permute-start = (bf16[3,2,256]{1,2,0:T(8,128)(2,1)}, bf16[3,2,256]{1,2,0:T(8,128)(2,1)}, u32[]{:S(2)}, u32[]{:S(2)}) collective-permute-start(bf16[3,2,256]{1,2,0:T(8,128)(2,1)} %copy.127), channel_id=1, source_target_pairs={{0,1},{1,2},{2,3},{3,4},{4,5},{5,6},{6,7},{7,8},{8,9},{9,10},{10,1... | collective-permute-start | bytes 9224 | tf_op jit(solution)/shard_map/ppermute | solution.py:13
  6.4 10.4 %copy-start.17 = (f32[16,16]{0,1:T(8,128)}, f32[16,16]{0,1:T(8,128)S(1)}, u32[]{:S(2)}) copy-start(f32[16,16]{0,1:T(8,128)S(1)} %copy.130) | copy-start | bytes 3076
  16.1 0.7 copy-start.19
  19.6 6.2 %copy-start.12 = (f32[1,16,16,128]{3,2,1,0:T(8,128)S(1)}, f32[1,16,16,128]{3,2,1,0:T(8,128)}, u32[]{:S(2)}) copy-start(f32[1,16,16,128]{3,2,1,0:T(8,128)} %negate_bitcast_fusion.1) | copy-start | bytes 393220
  19.6 6.2 %copy-start.13 = (f32[16,16,128]{2,1,0:T(8,128)S(1)}, f32[16,16,128]{2,1,0:T(8,128)}, u32[]{:S(2)}) copy-start(f32[16,16,128]{2,1,0:T(8,128)} %rev.24) | copy-start | bytes 393220
  19.6 6.9 %copy-start.14 = (f32[1,16,16,128]{3,2,0,1:T(8,128)S(1)}, f32[1,16,16,128]{3,2,0,1:T(8,128)}, u32[]{:S(2)}) copy-start(f32[1,16,16,128]{3,2,0,1:T(8,128)} %get-tuple-element.586) | copy-start | bytes 393220
  19.6 6.9 %copy-start.15 = (f32[1,16,16,128]{3,2,0,1:T(8,128)S(1)}, f32[1,16,16,128]{3,2,0,1:T(8,128)}, u32[]{:S(2)}) copy-start(f32[1,16,16,128]{3,2,0,1:T(8,128)} %get-tuple-element.587) | copy-start | bytes 393220
  19.7 7.6 %copy-start.28 = (f32[3,1,256]{2,1,0:T(1,128)S(1)}, f32[3,1,256]{2,1,0:T(1,128)}, u32[]{:S(2)}) copy-start(f32[3,1,256]{2,1,0:T(1,128)} %get-tuple-element.589) | copy-start | bytes 9220
  19.7 7.6 %copy-start.29 = (f32[3,1,256]{2,1,0:T(1,128)S(1)}, f32[3,1,256]{2,1,0:T(1,128)}, u32[]{:S(2)}) copy-start(f32[3,1,256]{2,1,0:T(1,128)} %get-tuple-element.590) | copy-start | bytes 9220
  19.7 8.2 %copy-start.22 = (pred[128,128]{1,0:T(8,128)(4,1)S(1)}, pred[128,128]{1,0:T(8,128)(4,1)}, u32[]{:S(2)}) copy-start(pred[128,128]{1,0:T(8,128)(4,1)} %fusion.89) | copy-start | bytes 49156
  26.6 6.2 %copy-start.27 = (f32[3,1,256]{2,1,0:T(1,128)S(1)}, f32[3,1,256]{2,1,0:T(1,128)}, u32[]{:S(2)}) copy-start(f32[3,1,256]{2,1,0:T(1,128)} %get-tuple-element.588) | copy-start | bytes 9220
  28.5 12.4 %copy-start.26 = (f32[16,16]{0,1:T(8,128)S(1)}, f32[16,16]{0,1:T(8,128)}, u32[]{:S(2)}) copy-start(f32[16,16]{0,1:T(8,128)} %get-tuple-element.597) | copy-start | bytes 3076
  52.5 1.8 copy-start
  52.5 1.4 copy-start.10
  54.3 1.0 copy-start.8
  208.1 13.3 %copy-start.9 = (f32[1024,256]{0,1:T(8,128)S(1)}, f32[1024,256]{0,1:T(8,128)}, u32[]{:S(2)}) copy-start(f32[1024,256]{0,1:T(8,128)} %copy-done.8) | copy-start | bytes 3145732
  229.5 61.0 %all-to-all-start = ((f32[16,1,5,16,256]{4,3,2,1,0:T(8,128)}), f32[16,1,5,16,256]{4,3,2,1,0:T(8,128)}, u32[]{:S(2)}, u32[]{:S(2)}) async-start(f32[16,1,5,16,256]{4,3,2,1,0:T(8,128)} %stack.71), calls=%async_computation | async-start | bytes 2621440 | tf_op jit(solution)/shard_map/all_to_all | solution.py:127
  288.1 4.0 copy-start.16
  288.1 4.0 copy-start.31
  288.1 4.0 copy-start.32
  288.1 4.0 copy-start.38
  290.5 3.8 copy-start.21
  290.5 3.8 copy-start.34
  290.5 3.8 copy-start.35
  290.5 3.9 copy-start.36
  290.5 3.9 copy-start.37
  292.0 3.4 copy-start.18
  292.0 3.4 copy-start.20
  294.6 102.7 %copy-start.1 = (f32[3,1024,256]{1,2,0:T(8,128)S(1)}, f32[3,1024,256]{1,2,0:T(8,128)}, u32[]{:S(2)}) copy-start(f32[3,1024,256]{1,2,0:T(8,128)} %copy-done) | copy-start | bytes 9437188
  399.2 4.7 %copy-start.2 = (f32[1,1024,256]{1,2,0:T(8,128)S(1)}, f32[1,1024,256]{1,2,0:T(8,128)}, u32[]{:S(2)}) copy-start(f32[1,1024,256]{1,2,0:T(8,128)} %get-tuple-element.574) | copy-start | bytes 3145732
  399.2 4.7 %copy-start.4 = (f32[1,1024,256]{1,2,0:T(8,128)S(1)}, f32[1,1024,256]{1,2,0:T(8,128)}, u32[]{:S(2)}) copy-start(f32[1,1024,256]{1,2,0:T(8,128)} %get-tuple-element.575) | copy-start | bytes 3145732
  403.9 1.0 copy-start.6
  403.9 5.6 %copy-start.11 = (bf16[1024,256]{0,1:T(8,128)(2,1)S(1)}, bf16[1024,256]{0,1:T(8,128)(2,1)}, u32[]{:S(2)}) copy-start(bf16[1024,256]{0,1:T(8,128)(2,1)} %get-tuple-element.579) | copy-start | bytes 1572868
  403.9 14.5 %copy-start.3 = (f32[1,1024,256]{1,2,0:T(8,128)S(1)}, f32[1,1024,256]{1,2,0:T(8,128)}, u32[]{:S(2)}) copy-start(f32[1,1024,256]{1,2,0:T(8,128)} %get-tuple-element.574) | copy-start | bytes 3145732
  403.9 14.5 %copy-start.5 = (f32[1,1024,256]{1,2,0:T(8,128)S(1)}, f32[1,1024,256]{1,2,0:T(8,128)}, u32[]{:S(2)}) copy-start(f32[1,1024,256]{1,2,0:T(8,128)} %get-tuple-element.575) | copy-start | bytes 3145732
  405.7 12.7 %collective-permute-start.1 = (f32[3,2,256]{1,2,0:T(8,128)}, f32[3,2,256]{1,2,0:T(8,128)}, u32[]{:S(2)}, u32[]{:S(2)}) collective-permute-start(f32[3,2,256]{1,2,0:T(8,128)} %slice.149), channel_id=1, source_target_pairs={{1,0},{2,1},{3,2},{4,3},{5,4},{6,5},{7,6},{8,7},{9,8},{10,9},{11,1... | collective-permute-start | bytes 18440 | tf_op jit(solution)/shard_map/ppermute | solution.py:13
  410.5 9.6 %copy-start.7 = (f32[1,1024,256]{1,2,0:T(8,128)S(1)}, f32[1,1024,256]{1,2,0:T(8,128)}, u32[]{:S(2)}) copy-start(f32[1,1024,256]{1,2,0:T(8,128)} %copy-done.6) | copy-start | bytes 3145732
  410.5 9.6 %copy-start.23 = (f32[3,256]{1,0:T(4,128)S(1)}, f32[3,256]{1,0:T(4,128)}, u32[]{:S(2)}) copy-start(f32[3,256]{1,0:T(4,128)} %get-tuple-element.603) | copy-start | bytes 9220
  410.5 9.6 %copy-start.24 = (f32[3,256]{1,0:T(4,128)S(1)}, f32[3,256]{1,0:T(4,128)}, u32[]{:S(2)}) copy-start(f32[3,256]{1,0:T(4,128)} %get-tuple-element.604) | copy-start | bytes 9220
  410.5 9.6 %copy-start.25 = (f32[3,1,256]{2,0,1:T(4,128)S(1)}, f32[3,1,256]{2,0,1:T(4,128)}, u32[]{:S(2)}) copy-start(f32[3,1,256]{2,0,1:T(4,128)} %copy.197) | copy-start | bytes 9220
